TPU v7x, 256 devices: a whole 4x4x8 slice. The times are simulated.
256 devices in a mesh: dp: 8 (over y, core), expert: 32 (over x, z).
Axes of the slice: x: 4, y: 4, z: 8, core: 2. Of those that a mesh axis runs over, the one named last changes fastest.
Arguments:
- tokens: bfloat16 [2048, 3584], P(('dp', 'expert')), may hold values from -6 to 6
- routes: int32 [2048, 8], P(('dp', 'expert')), may hold values from 0 to 63, all different within a row; in each aligned block of 8 rows (0 to 7, 8 to 15, ...) at most 2 rows name the same one
- gates: bfloat16 [2048, 8], P(('dp', 'expert')), may hold values from 0.049804688 to 0.5
- cotangent: bfloat16 [2048, 3584], P(('dp', 'expert')), may hold values from -1.5 to 1.5
- w_gate: bfloat16 [64, 3584, 1024], P('expert', None, 'dp'), may hold values from -0.09375 to 0.09375
- w_up: bfloat16 [64, 3584, 1024], P('expert', None, 'dp'), may hold values from -0.09375 to 0.09375
- w_down: bfloat16 [64, 1024, 3584], P('expert', 'dp'), may hold values from -0.1875 to 0.1875
Outputs:
- token_grads: bfloat16 [2048, 3584], P(('dp', 'expert'))
- gate_grads: float32 [2048, 8], P(('dp', 'expert'))
- grad_gate: bfloat16 [64, 3584, 1024], P('expert', None, 'dp')
- grad_up: bfloat16 [64, 3584, 1024], P('expert', None, 'dp')
- grad_down: bfloat16 [64, 1024, 3584], P('expert', 'dp')
Inputs may be any that keep to these rules, and one draw needn't show every extreme that they name: `routes`: each row names 8 different experts. Within each device's block of 8 rows no expert is named by more than 2 rows, a bound that some block reaches.
All inputs are finite; a program needn't handle non-finite values.
Results may differ from a plain program's by a relative error of at most 0.0058.
Values may be sent and summed in bfloat16 or wider, within the bound.
A program may use at most 192 MiB of HBM per device.

v0:
```python
from functools import partial
import jax
import jax.numpy as jnp
from jax import lax
from jax.sharding import PartitionSpec as P

TOPK = 8


def route_table(routes, experts_all, capacity):
    pairs = routes.reshape(-1)
    onehot = (pairs[:, None] == jnp.arange(experts_all, dtype=jnp.int32)[None, :]).astype(jnp.int32)
    before = jnp.cumsum(onehot, axis=0) - onehot
    within = jnp.sum(before * onehot, axis=1)
    target = pairs * capacity + within
    slot_ids = jnp.arange(experts_all * capacity, dtype=jnp.int32)
    return (target[:, None] == slot_ids[None, :]).astype(jnp.float32)


def dispatch(table, tokens, cotangent, gates):
    count = tokens.shape[0]
    slots = table.shape[1]
    spread = table.reshape(count, TOPK, slots).sum(axis=1).astype(jnp.bfloat16)
    both = jnp.concatenate([tokens, cotangent], axis=1)
    slot_rows = jnp.einsum("ts,td->sd", spread, both, preferred_element_type=jnp.float32).astype(
        jnp.bfloat16
    )
    flat_gates = gates.reshape(-1).astype(jnp.float32)
    slot_gates = jnp.einsum("ps,p->s", table, flat_gates, precision=lax.Precision.HIGHEST).astype(
        jnp.bfloat16
    )
    pad = jnp.zeros((slots, 127), jnp.bfloat16)
    return jnp.concatenate([slot_rows, slot_gates[:, None], pad], axis=1)


def expert_one(rows_in, cot_in, row_gate, w_gate, w_up, w_down):
    gate_pre = jnp.dot(rows_in, w_gate, preferred_element_type=jnp.float32)
    upper_pre = jnp.dot(rows_in, w_up, preferred_element_type=jnp.float32)
    gate_sig = jax.nn.sigmoid(gate_pre)
    active = (gate_pre * gate_sig * upper_pre).astype(jnp.bfloat16)
    output = jnp.dot(active, w_down, preferred_element_type=jnp.float32)
    cot_float = cot_in.astype(jnp.float32)
    gate_part = jnp.sum(output * cot_float, axis=-1)
    scaled = (row_gate.astype(jnp.float32)[:, None] * cot_float).astype(jnp.bfloat16)
    grad_active = lax.dot_general(
        scaled, w_down, (((1,), (1,)), ((), ())), preferred_element_type=jnp.float32
    )
    grad_upper = (grad_active * gate_pre * gate_sig).astype(jnp.bfloat16)
    grad_gpre = (grad_active * upper_pre * gate_sig * (1.0 + gate_pre * (1.0 - gate_sig))).astype(
        jnp.bfloat16
    )
    token_part = lax.dot_general(
        grad_gpre, w_gate, (((1,), (1,)), ((), ())), preferred_element_type=jnp.float32
    )
    token_part = token_part + lax.dot_general(
        grad_upper, w_up, (((1,), (1,)), ((), ())), preferred_element_type=jnp.float32
    )
    grad_g = lax.dot_general(
        rows_in, grad_gpre, (((0,), (0,)), ((), ())), preferred_element_type=jnp.float32
    ).astype(jnp.bfloat16)
    grad_u = lax.dot_general(
        rows_in, grad_upper, (((0,), (0,)), ((), ())), preferred_element_type=jnp.float32
    ).astype(jnp.bfloat16)
    grad_d = lax.dot_general(
        active, scaled, (((0,), (0,)), ((), ())), preferred_element_type=jnp.float32
    ).astype(jnp.bfloat16)
    return (token_part, gate_part, grad_g, grad_u, grad_d)


def local(tokens, routes, gates, cotangent, w_gate, w_up, w_down):
    n_expert = lax.axis_size("expert")
    n_groups = lax.axis_size("dp")
    local_experts = w_gate.shape[0]
    experts_all = local_experts * n_expert
    tok_count = tokens.shape[0]
    width = tokens.shape[1]
    capacity = 16 * tok_count // experts_all
    slots = experts_all * capacity
    per_dest = local_experts * capacity
    table = route_table(routes, experts_all, capacity)
    send = dispatch(table, tokens, cotangent, gates)
    send = send.reshape(n_expert, per_dest, send.shape[-1])
    recv = lax.all_to_all(send, "expert", split_axis=0, concat_axis=0, tiled=True)
    recv = lax.all_gather(recv, "dp", axis=0, tiled=True)
    rows = n_groups * n_expert
    parts, gparts, grads_g, grads_u, grads_d = ([], [], [], [], [])
    for j in range(local_experts):
        block = recv[:, j * capacity : (j + 1) * capacity, :].reshape(rows * capacity, -1)
        token_part, gate_part, grad_g, grad_u, grad_d = expert_one(
            block[:, :width],
            block[:, width : 2 * width],
            block[:, 2 * width],
            w_gate[j],
            w_up[j],
            w_down[j],
        )
        token_part = token_part.reshape(n_groups, n_expert * capacity, width)
        part = lax.psum_scatter(token_part, "dp", scatter_dimension=0, tiled=False)
        parts.append(part.reshape(n_expert, capacity, width))
        gparts.append(gate_part.reshape(n_groups, n_expert, capacity))
        grads_g.append(grad_g)
        grads_u.append(grad_u)
        grads_d.append(grad_d)
    token_part = jnp.stack(parts, axis=1).reshape(n_expert, local_experts, capacity, width)
    gate_part = jnp.stack(gparts, axis=2).reshape(n_groups, n_expert * per_dest)
    gate_part = lax.psum_scatter(gate_part, "dp", scatter_dimension=0, tiled=False)
    gate_part = gate_part.reshape(n_expert, per_dest)
    back_tokens, back_gates = (
        lax.all_to_all(token_part, "expert", split_axis=0, concat_axis=0, tiled=True),
        lax.all_to_all(gate_part, "expert", split_axis=0, concat_axis=0, tiled=True),
    )
    back_tokens = back_tokens.reshape(slots, width)
    back_gates = back_gates.reshape(slots)
    spread = table.reshape(tok_count, TOPK, slots).sum(axis=1)
    token_sum = jnp.einsum("ts,sd->td", spread, back_tokens, precision=lax.Precision.HIGHEST)
    gate_sum = jnp.einsum("ps,s->p", table, back_gates, precision=lax.Precision.HIGHEST)
    token_grads = token_sum.astype(jnp.bfloat16)
    gate_grads = gate_sum.reshape(tok_count, TOPK)
    grad_gate = jnp.stack(grads_g, axis=0)
    grad_up = jnp.stack(grads_u, axis=0)
    grad_down = jnp.stack(grads_d, axis=0)
    return (token_grads, gate_grads, grad_gate, grad_up, grad_down)


def solution(mesh):
    return jax.shard_map(
        local,
        mesh=mesh,
        in_specs=(
            P(("dp", "expert"), None),
            P(("dp", "expert"), None),
            P(("dp", "expert"), None),
            P(("dp", "expert"), None),
            P("expert", None, "dp"),
            P("expert", None, "dp"),
            P("expert", "dp", None),
        ),
        out_specs=(
            P(("dp", "expert"), None),
            P(("dp", "expert"), None),
            P("expert", None, "dp"),
            P("expert", None, "dp"),
            P("expert", "dp", None),
        ),
        check_vma=False,
    )
```

profile of v0, /device:TPU:32, one launch (start us, length us, event | category | flops | bytes accessed | tf_op | source)
XLA Modules:
  0.0 374.6 jit_solution(2525341771582631884)
XLA Ops:
  7.2 0.8 eq.57
  8.4 0.7 multiply_add_fusion
  10.4 1.5 convolution_convert_fusion
  11.9 1.6 concatenate.12
  14.1 5.0 %concatenate.14 = bf16[32,4,7296]{2,1,0:T(4,128)(2,1)S(1)} concatenate(bf16[32,4,7168]{2,1,0:T(4,128)(2,1)} %concatenate.12, bf16[32,4,1]{2,1,0:T(4,128)(2,1)S(1)} %concatenate.15, bf16[32,4,127]{2,1,0:T(4,128)(2,1)S(1)} %broadcast_in_dim.2), dimensions={2} | concatenate | bytes 3735552 | tf_op jit(solution)/shard_map/concatenate | solution.py:33
  19.1 57.3 %all_to_all.19 = bf16[32,4,7296]{2,1,0:T(4,128)(2,1)} all-to-all(bf16[32,4,7296]{2,1,0:T(4,128)(2,1)S(1)} %concatenate.14), channel_id=1, replica_groups=mesh['dp'=8,'expert'=32] {'expert'}, dimensions={0} | all-to-all | bytes 3735552 | tf_op jit(solution)/shard_map/all_to_all | solution.py:83
  76.5 76.3 %all-gather.2.cloned.1.call-done = bf16[256,4,7296]{2,1,0:T(4,128)(2,1)} async-done(((bf16[32,4,7296]{2,1,0:T(4,128)(2,1)}), bf16[256,4,7296]{2,1,0:T(4,128)(2,1)}) %all-gather.2.cloned.1.call-update) | async-done | bytes 14942224 | tf_op jit(solution)/shard_map/all_gather | solution.py:84
  152.8 16.6 %fusion.66 = (bf16[256,2,7296]{2,1,0:T(2,128)(2,1)}, bf16[256,2,7296]{2,1,0:T(2,128)(2,1)}) fusion(bf16[256,4,7296]{2,1,0:T(4,128)(2,1)} %all-gather.2.cloned.1.call-done), kind=kLoop, calls=%fused_computation.100 | loop fusion | bytes 29884416 | tf_op jit(solution)/shard_map/slice | solution.py:88
  169.4 15.7 %reshape.89 = bf16[512,7296]{1,0:T(8,128)(2,1)} reshape(bf16[256,2,7296]{2,1,0:T(2,128)(2,1)} %get-tuple-element.5) | data formatting | bytes 14942208 | tf_op jit(solution)/shard_map/reshape | solution.py:88
  185.1 1.2 convert_reduce_fusion.1
  186.3 3.3 fusion.18
  189.7 3.4 fusion.27
  193.2 1.1 multiply_convert_fusion.1
  194.3 1.1 fusion.36
  195.5 4.1 %convolution_add_fusion.1 = f32[512,3584]{1,0:T(8,128)} fusion(f32[512,3584]{1,0:T(8,128)S(1)} %fusion.36, bf16[512,128]{1,0:T(8,128)(2,1)S(1)} %get-tuple-element.9, bf16[2,3584,128]{2,1,0:T(8,128)(2,1)S(1)} %copy-done.1), kind=kOutput, calls=%fused_computation.10 | convolution fusion | flops 471597056 | bytes 15728640 | tf_op jit(solution)/shard_map/dot_general | solution.py:55
  199.8 15.7 %reshape.91 = bf16[512,7296]{1,0:T(8,128)(2,1)} reshape(bf16[256,2,7296]{2,1,0:T(2,128)(2,1)} %get-tuple-element.6) | data formatting | bytes 14942208 | tf_op jit(solution)/shard_map/reshape | solution.py:88
  215.5 1.2 convert_reduce_fusion
  216.7 3.4 fusion.12
  220.1 3.4 fusion.24
  223.8 1.1 multiply_convert_fusion
  225.0 1.1 fusion.29
  226.1 4.1 %convolution_add_fusion = f32[512,3584]{1,0:T(8,128)} fusion(f32[512,3584]{1,0:T(8,128)S(1)} %fusion.29, bf16[512,128]{1,0:T(8,128)(2,1)S(1)} %get-tuple-element.12, bf16[2,3584,128]{2,1,0:T(8,128)(2,1)S(1)} %copy-done.2), kind=kOutput, calls=%fused_computation.9 | convolution fusion | flops 471597056 | bytes 15728640 | tf_op jit(solution)/shard_map/dot_general | solution.py:55
  230.2 0.6 copy-done.18
  231.8 3.3 fusion.1
  235.2 3.3 fusion.3
  239.2 25.2 %all-reduce = f32[8,128]{0,1:T(8,128)S(1)} all-reduce(f32[8,128]{0,1:T(8,128)S(1)} %bitcast.88), channel_id=4, replica_groups=mesh['dp'=8,'expert'=32] {'dp'}, use_global_device_ids=true, to_apply=%region_7.8.clone | all-reduce | flops 1024 | bytes 8192
  264.4 0.8 dynamic-slice_reduce_fusion
  265.2 0.7 all_to_all.14
  266.0 10.1 %all-to-all-start.2 = ((f32[32,1,4]{2,1,0:T(1,128)}), f32[32,1,4]{2,1,0:T(1,128)S(1)}, u32[]{:S(2)}, u32[]{:S(2)}) async-start(f32[32,1,4]{2,1,0:T(1,128)} %bitcast.11), calls=%async_computation.4 | async-start | bytes 32768 | tf_op jit(solution)/shard_map/all_to_all | solution.py:110
  276.1 2.7 stack_reshape_reduce_scatter.6
  278.7 24.2 %reduce-scatter.6.cloned.1.call-done = f32[1,64,3584]{2,1,0:T(8,128)} async-done(((f32[8,64,3584]{2,1,0:T(8,128)}), f32[1,64,3584]{2,1,0:T(8,128)}) %reduce-scatter.6.cloned.1.call-update) | async-done | bytes 917520 | tf_op jit(solution)/shard_map/reduce_scatter | solution.py:98
  302.9 2.6 stack_reshape_reduce_scatter.7
  305.6 3.8 %pad_maximum_fusion = f32[32,2,2,3584]{3,2,1,0:T(2,128)} fusion(f32[32,1,2,3584]{3,2,1,0:T(2,128)} %stack_reshape_reduce_scatter.7, f32[32,1,2,3584]{3,2,1,0:T(2,128)} %stack_reshape_reduce_scatter.6), kind=kLoop, calls=%fused_computation.36 | loop fusion | flops 458752 | bytes 3670016 | tf_op jit(solution)/shard_map/stack | solution.py:104
  309.3 10.3 %all-to-all-start.1 = ((f32[32,2,2,3584]{3,2,1,0:T(2,128)}), f32[32,2,2,3584]{3,2,1,0:T(2,128)}, u32[]{:S(2)}, u32[]{:S(2)}) async-start(f32[32,2,2,3584]{3,2,1,0:T(2,128)} %pad_maximum_fusion), calls=%async_computation.3 | async-start | bytes 3670016 | tf_op jit(solution)/shard_map/all_to_all | solution.py:109
  319.7 3.4 fusion.6
  323.1 1.2 fusion.4
  324.3 1.2 slice-done.7
  325.5 1.2 fusion.5
  326.7 1.2 fusion.7
  327.9 0.9 fusion.8
  328.8 1.0 fusion.9
  329.8 1.4 pad_maximum_fusion.3
  331.2 2.2 pad_maximum_fusion.1
  333.9 0.7 reduce.9
  334.7 1.0 fusion.60
  335.7 28.2 %all-to-all-done.1 = f32[32,2,2,3584]{3,2,1,0:T(2,128)} async-done(((f32[32,2,2,3584]{3,2,1,0:T(2,128)}), f32[32,2,2,3584]{3,2,1,0:T(2,128)}, u32[]{:S(2)}, u32[]{:S(2)}) %all-to-all-start.1) | async-done | bytes 1835040 | tf_op jit(solution)/shard_map/all_to_all | solution.py:109
  363.9 2.6 reshape.93
  366.4 1.6 convolution_convert_fusion.7
  (89 shorter events, 5.4 us)
Async XLA Ops:
  7.2 6.4 %copy-start.14 = (bf16[8,8]{1,0:T(8,128)(2,1)S(1)}, bf16[8,8]{1,0:T(8,128)(2,1)}, u32[]{:S(2)}) copy-start(bf16[8,8]{1,0:T(8,128)(2,1)} %param.9) | copy-start | bytes 388
  7.2 145.6 %all-gather.2.cloned.1.call-start = ((), (), s32[]{:S(2)}) async-start(), calls=%async_computation.5 | async-start | bytes 16809984 | tf_op jit(solution)/shard_map/all_gather | solution.py:84
  9.1 0.6 copy-start.8
  9.8 0.6 copy-start.6
  76.4 199.6 %reduce-scatter.4.cloned.1.call-start = ((), (), s32[]{:S(2)}) async-start(), calls=%async_computation.6 | async-start | bytes 8257536 | tf_op jit(solution)/shard_map/reduce_scatter | solution.py:98
  169.4 16.9 %copy-start = (bf16[2,3584,128]{2,1,0:T(8,128)(2,1)S(1)}, bf16[2,3584,128]{2,1,0:T(8,128)(2,1)}, u32[]{:S(2)}) copy-start(bf16[2,3584,128]{2,1,0:T(8,128)(2,1)} %param.11) | copy-start | bytes 5505028
  185.1 4.5 %copy-start.15 = (bf16[2,128,3584]{2,1,0:T(8,128)(2,1)S(1)}, bf16[2,128,3584]{2,1,0:T(8,128)(2,1)}, u32[]{:S(2)}) copy-start(bf16[2,128,3584]{2,1,0:T(8,128)(2,1)} %param.13) | copy-start | bytes 5505028
  186.3 6.7 %copy-start.10 = (f32[512]{0:T(512)}, f32[512]{0:T(512)S(1)}, u32[]{:S(2)}) copy-start(f32[512]{0:T(512)S(1)} %convert_reduce_fusion.1) | copy-start | bytes 6148
  186.3 6.7 %slice-start = ((s8[7471104]{0:T(1024)(128)(4,1)}), s8[4194304]{0:T(1024)(128)(4,1)S(1)}, s32[]{:S(2)}) async-start(s8[7471104]{0:T(1024)(128)(4,1)} %bitcast.80), calls=%async_computation.8 | async-start | bytes 8388608
  189.6 3.4 slice-start.1
  189.7 3.5 copy-start.1
  194.3 1.1 copy-start.3
  194.3 37.1 %copy-start.19 = (bf16[512,128]{1,0:T(8,128)(2,1)}, bf16[512,128]{1,0:T(8,128)(2,1)S(1)}, u32[]{:S(2)}) copy-start(bf16[512,128]{1,0:T(8,128)(2,1)S(1)} %get-tuple-element.7) | copy-start | bytes 393220
  199.6 103.3 %reduce-scatter.6.cloned.1.call-start = ((), (), s32[]{:S(2)}) async-start(), calls=%async_computation.7 | async-start | bytes 8257536 | tf_op jit(solution)/shard_map/reduce_scatter | solution.py:98
  215.5 4.6 %copy-start.16 = (bf16[2,128,3584]{2,1,0:T(8,128)(2,1)S(1)}, bf16[2,128,3584]{2,1,0:T(8,128)(2,1)}, u32[]{:S(2)}) copy-start(bf16[2,128,3584]{2,1,0:T(8,128)(2,1)} %param.13) | copy-start | bytes 5505028
  216.7 3.4 copy-start.12
  216.7 6.9 %slice-start.4 = ((s8[7471104]{0:T(1024)(128)(4,1)}), s8[4194304]{0:T(1024)(128)(4,1)S(1)}, s32[]{:S(2)}) async-start(s8[7471104]{0:T(1024)(128)(4,1)} %bitcast.84), calls=%async_computation.12 | async-start | bytes 8388608
  220.1 3.5 slice-start.5
  220.1 3.8 %copy-start.2 = (bf16[2,3584,128]{2,1,0:T(8,128)(2,1)S(1)}, bf16[2,3584,128]{2,1,0:T(8,128)(2,1)}, u32[]{:S(2)}) copy-start(bf16[2,3584,128]{2,1,0:T(8,128)(2,1)} %param.12) | copy-start | bytes 5505028
  225.0 1.1 copy-start.4
  225.0 10.2 %copy-start.21 = (bf16[512,128]{1,0:T(8,128)(2,1)}, bf16[512,128]{1,0:T(8,128)(2,1)S(1)}, u32[]{:S(2)}) copy-start(bf16[512,128]{1,0:T(8,128)(2,1)S(1)} %get-tuple-element.10) | copy-start | bytes 393220
  230.2 0.7 copy-start.18
  230.2 1.6 copy-start.17
  266.0 43.4 %all-to-all-start.2 = ((f32[32,1,4]{2,1,0:T(1,128)}), f32[32,1,4]{2,1,0:T(1,128)S(1)}, u32[]{:S(2)}, u32[]{:S(2)}) async-start(f32[32,1,4]{2,1,0:T(1,128)} %bitcast.11), calls=%async_computation.4 | async-start | bytes 32768 | tf_op jit(solution)/shard_map/all_to_all | solution.py:110
  305.6 17.5 %slice-start.2 = ((s8[7471104]{0:T(1024)(128)(4,1)}), s8[3276800]{0:T(1024)(128)(4,1)S(1)}, s32[]{:S(2)}) async-start(s8[7471104]{0:T(1024)(128)(4,1)} %bitcast.82), calls=%async_computation.10 | async-start | bytes 6553600
  309.3 54.5 %all-to-all-start.1 = ((f32[32,2,2,3584]{3,2,1,0:T(2,128)}), f32[32,2,2,3584]{3,2,1,0:T(2,128)}, u32[]{:S(2)}, u32[]{:S(2)}) async-start(f32[32,2,2,3584]{3,2,1,0:T(2,128)} %pad_maximum_fusion), calls=%async_computation.3 | async-start | bytes 3670016 | tf_op jit(solution)/shard_map/all_to_all | solution.py:109
  319.7 3.4 slice-start.3
  319.7 4.6 %slice-start.6 = ((s8[7471104]{0:T(1024)(128)(4,1)}), s8[4194304]{0:T(1024)(128)(4,1)S(1)}, s32[]{:S(2)}) async-start(s8[7471104]{0:T(1024)(128)(4,1)} %bitcast.86), calls=%async_computation.14 | async-start | bytes 8388608
  323.1 2.4 slice-start.7
  325.5 1.2 copy-start.5
  326.6 1.2 copy-start.11
  326.7 1.2 copy-start.20
  327.9 0.9 copy-start.13
  327.9 0.9 copy-start.22
  331.2 3.5 copy-start.9
  333.3 33.1 %copy-start.7 = (f32[8,128]{1,0:T(8,128)S(1)}, f32[8,128]{1,0:T(8,128)}, u32[]{:S(2)}) copy-start(f32[8,128]{1,0:T(8,128)} %copy-done.6) | copy-start | bytes 12292
Sparse Core Ops, SparseCore 0:
  76.6 76.1 all-gather.1
  199.7 50.7 reduce-scatter.3
  253.0 49.8 reduce-scatter.5
where the time goes:
time: 376 us; the launch traced here: 375 us
  waiting for transfers between devices  129 us (34%)
  blocking collectives  82.5 us (22%)
  local copies, waits for them, and re-layouts  71 us (19%)
  matrix products  45.7 us (12%)
  starting transfers between devices  20.7 us (6%)
  between operations  14.3 us (4%)
  other arithmetic  11.5 us (3%)
    all_gather x1, waiting for transfers between devices, local(): recv = lax.all_gather(recv, 'dp', axis=0, tiled=True)  76.3 us
    all_to_all x1, blocking collectives, local(): lax.all_to_all(send, 'expert', split_axis=0, concat_axis=0, tiled=True)  57.3 us
    reshape x2, local copies, waits for them, and re-layouts, local(): recv[:, j * capacity:(j + 1) * capacity, :].reshape(rows * capacity, -1)  31.4 us
    all_to_all x1, waiting for transfers between devices, local(): lax.all_to_all(token_part, 'expert', split_axis=0, concat_axis=0, tiled=T...  28.2 us
    unnamed x1, blocking collectives  25.2 us
    reduce_scatter x2, waiting for transfers between devices, local(): part = lax.psum_scatter(token_part, 'dp', scatter_dimension=0, tiled=False)  24.2 us
    slice x1, local copies, waits for them, and re-layouts, local(): recv[:, j * capacity:(j + 1) * capacity, :].reshape(rows * capacity, -1)  16.6 us
    all_to_all x1, starting transfers between devices, local(): lax.all_to_all(token_part, 'expert', split_axis=0, concat_axis=0, tiled=T...  10.3 us
  transfers between devices with their start and end apart: 5, of which 3 were waited for; matrix products, arithmetic and copies ran while one was open for 17% of the time, Pallas kernels for 0%

commit v1 on v0

--- a/solution.py
+++ b/solution.py
@@ -81,7 +81,9 @@
     send = dispatch(table, tokens, cotangent, gates)
     send = send.reshape(n_expert, per_dest, send.shape[-1])
     recv = lax.all_to_all(send, "expert", split_axis=0, concat_axis=0, tiled=True)
-    recv = lax.all_gather(recv, "dp", axis=0, tiled=True)
+    recv = jnp.concatenate(
+        lax.all_to_all(jnp.stack([recv] * lax.axis_size("dp")), "dp", 0, 0), axis=0
+    )
     rows = n_groups * n_expert
     parts, gparts, grads_g, grads_u, grads_d = ([], [], [], [], [])
     for j in range(local_experts):

time: 376 us -> 469 us (1.25)
  blocking collectives: 82.5 us -> 251 us
  waiting for transfers between devices: 129 us -> 53.7 us
  starting transfers between devices: 20.7 us -> 15.7 us
    all_to_all x0 -> x1, blocking collectives: none -> 169 us  [local(): lax.all_to_all(jnp.stack([recv] * lax.axis_size('dp')), 'dp', 0, 0)]
    all_gather x1 -> x0, waiting for transfers between devices: 76.3 us -> none  [local(): recv = lax.all_gather(recv, 'dp', axis=0, tiled=True)]
    all_to_all x1, starting transfers between devices: 10.1 us -> 5.17 us  [local(): lax.all_to_all(gate_part, 'expert', split_axis=0, concat_axis=0, tiled=True)]
  transfers between devices with their start and end apart: 5 -> 4, of which waited for: 3 -> 2; matrix products, arithmetic and copies ran while one was open for 17% -> 13% of each run, Pallas kernels for 0% -> 0%
where the time goes in v1:
time: 469 us; the launch traced here: 468 us
  blocking collectives  251 us (54%)
  local copies, waits for them, and re-layouts  75.5 us (16%)
  waiting for transfers between devices  53.7 us (11%)
  matrix products  45.7 us (10%)
  starting transfers between devices  15.7 us (3%)
  between operations  14.6 us (3%)
  other arithmetic  11.5 us (2%)
    all_to_all x1, blocking collectives, local(): lax.all_to_all(jnp.stack([recv] * lax.axis_size('dp')), 'dp', 0, 0)  169 us
    all_to_all x1, blocking collectives, local(): lax.all_to_all(send, 'expert', split_axis=0, concat_axis=0, tiled=True)  57.2 us
    reshape x2, local copies, waits for them, and re-layouts, local(): recv[:, j * capacity:(j + 1) * capacity, :].reshape(rows * capacity, -1)  31.4 us
    all_to_all x1, waiting for transfers between devices, local(): lax.all_to_all(token_part, 'expert', split_axis=0, concat_axis=0, tiled=T...  28.2 us
    reduce_scatter x2, waiting for transfers between devices, local(): part = lax.psum_scatter(token_part, 'dp', scatter_dimension=0, tiled=False)  25.5 us
    unnamed x1, blocking collectives  24.4 us
    slice x1, local copies, waits for them, and re-layouts, local(): recv[:, j * capacity:(j + 1) * capacity, :].reshape(rows * capacity, -1)  16.5 us
    all_to_all x1, starting transfers between devices, local(): lax.all_to_all(token_part, 'expert', split_axis=0, concat_axis=0, tiled=T...  10.3 us
  transfers between devices with their start and end apart: 4, of which 2 were waited for; matrix products, arithmetic and copies ran while one was open for 13% of the time, Pallas kernels for 0%

profile of v1, /device:TPU:32, one launch (start us, length us, event | category | flops | bytes accessed | tf_op | source)
XLA Modules:
  0.0 467.5 jit_solution(10736302597373295422)
XLA Ops:
  7.2 0.8 eq.57
  8.4 0.7 multiply_add_fusion
  10.4 1.5 convolution_convert_fusion
  11.9 1.6 concatenate.12
  14.1 5.0 %concatenate.14 = bf16[32,4,7296]{2,1,0:T(4,128)(2,1)S(1)} concatenate(bf16[32,4,7168]{2,1,0:T(4,128)(2,1)} %concatenate.12, bf16[32,4,1]{2,1,0:T(4,128)(2,1)S(1)} %concatenate.15, bf16[32,4,127]{2,1,0:T(4,128)(2,1)S(1)} %broadcast_in_dim.2), dimensions={2} | concatenate | bytes 3735552 | tf_op jit(solution)/shard_map/concatenate | solution.py:33
  19.1 57.2 %all_to_all.24 = bf16[32,4,7296]{2,1,0:T(4,128)(2,1)S(1)} all-to-all(bf16[32,4,7296]{2,1,0:T(4,128)(2,1)S(1)} %concatenate.14), channel_id=1, replica_groups=mesh['dp'=8,'expert'=32] {'expert'}, dimensions={0} | all-to-all | bytes 3735552 | tf_op jit(solution)/shard_map/all_to_all | solution.py:83
  76.3 4.6 stack.44
  80.9 169.2 %all_to_all.25 = bf16[8,32,4,7296]{3,2,1,0:T(4,128)(2,1)} all-to-all(bf16[8,32,4,7296]{3,2,1,0:T(4,128)(2,1)S(1)} %stack.44), channel_id=1, replica_groups=mesh['dp'=8,'expert'=32] {'dp'}, dimensions={0} | all-to-all | bytes 29884416 | tf_op jit(solution)/shard_map/all_to_all | solution.py:85
  250.1 16.5 %fusion.66 = (bf16[256,2,7296]{2,1,0:T(2,128)(2,1)}, bf16[256,2,7296]{2,1,0:T(2,128)(2,1)}) fusion(bf16[256,4,7296]{2,1,0:T(4,128)(2,1)} %bitcast.79), kind=kLoop, calls=%fused_computation.100 | loop fusion | bytes 29884416 | tf_op jit(solution)/shard_map/slice | solution.py:90
  266.6 15.7 %reshape.95 = bf16[512,7296]{1,0:T(8,128)(2,1)} reshape(bf16[256,2,7296]{2,1,0:T(2,128)(2,1)} %get-tuple-element.5) | data formatting | bytes 14942208 | tf_op jit(solution)/shard_map/reshape | solution.py:90
  282.4 1.2 convert_reduce_fusion.1
  283.5 3.3 fusion.18
  286.9 3.4 fusion.27
  290.4 1.1 multiply_convert_fusion.1
  291.6 1.1 fusion.36
  292.7 4.1 convolution_add_fusion.1
  297.0 15.7 %reshape.97 = bf16[512,7296]{1,0:T(8,128)(2,1)} reshape(bf16[256,2,7296]{2,1,0:T(2,128)(2,1)} %get-tuple-element.6) | data formatting | bytes 14942208 | tf_op jit(solution)/shard_map/reshape | solution.py:90
  312.7 1.2 convert_reduce_fusion
  313.9 3.4 fusion.12
  317.3 3.4 fusion.24
  321.0 1.1 multiply_convert_fusion
  322.2 1.1 fusion.29
  323.3 4.1 convolution_add_fusion
  328.9 3.3 fusion.1
  332.4 3.3 fusion.3
  336.4 24.4 %all-reduce = f32[8,128]{0,1:T(8,128)S(1)} all-reduce(f32[8,128]{0,1:T(8,128)S(1)} %bitcast.90), channel_id=4, replica_groups=mesh['dp'=8,'expert'=32] {'dp'}, use_global_device_ids=true, to_apply=%region_7.8.clone | all-reduce | flops 1024 | bytes 8192
  360.8 0.8 dynamic-slice_reduce_fusion
  361.6 0.7 all_to_all.18
  362.3 5.2 %all-to-all-start.3 = ((f32[32,1,4]{2,1,0:T(1,128)}), f32[32,1,4]{2,1,0:T(1,128)S(1)}, u32[]{:S(2)}, u32[]{:S(2)}) async-start(f32[32,1,4]{2,1,0:T(1,128)} %bitcast.12), calls=%async_computation.5 | async-start | bytes 32768 | tf_op jit(solution)/shard_map/all_to_all | solution.py:112
  367.5 2.6 stack_reshape_reduce_scatter.6
  370.2 25.4 %reduce-scatter.6.cloned.1.call-done = f32[1,64,3584]{2,1,0:T(8,128)} async-done(((f32[8,64,3584]{2,1,0:T(8,128)}), f32[1,64,3584]{2,1,0:T(8,128)}) %reduce-scatter.6.cloned.1.call-update) | async-done | bytes 917520 | tf_op jit(solution)/shard_map/reduce_scatter | solution.py:100
  395.6 2.6 stack_reshape_reduce_scatter.7
  398.3 3.8 pad_maximum_fusion
  402.1 10.3 %all-to-all-start.2 = ((f32[32,2,2,3584]{3,2,1,0:T(2,128)}), f32[32,2,2,3584]{3,2,1,0:T(2,128)}, u32[]{:S(2)}, u32[]{:S(2)}) async-start(f32[32,2,2,3584]{3,2,1,0:T(2,128)} %pad_maximum_fusion), calls=%async_computation.4 | async-start | bytes 3670016 | tf_op jit(solution)/shard_map/all_to_all | solution.py:111
  412.4 3.4 fusion.6
  415.8 1.2 fusion.4
  417.0 1.2 slice-done.7
  418.1 1.2 fusion.5
  419.3 1.2 fusion.7
  420.5 0.9 fusion.8
  421.5 1.0 fusion.9
  422.5 1.4 pad_maximum_fusion.3
  423.9 2.2 pad_maximum_fusion.1
  426.5 0.7 reduce.9
  427.3 1.0 fusion.60
  428.3 28.2 %all-to-all-done.2 = f32[32,2,2,3584]{3,2,1,0:T(2,128)} async-done(((f32[32,2,2,3584]{3,2,1,0:T(2,128)}), f32[32,2,2,3584]{3,2,1,0:T(2,128)}, u32[]{:S(2)}, u32[]{:S(2)}) %all-to-all-start.2) | async-done | bytes 1835040 | tf_op jit(solution)/shard_map/all_to_all | solution.py:111
  456.5 2.6 reshape.99
  459.1 1.6 convolution_convert_fusion.7
  (88 shorter events, 6.0 us)
Async XLA Ops:
  7.2 6.4 %copy-start.14 = (bf16[8,8]{1,0:T(8,128)(2,1)S(1)}, bf16[8,8]{1,0:T(8,128)(2,1)}, u32[]{:S(2)}) copy-start(bf16[8,8]{1,0:T(8,128)(2,1)} %param.9) | copy-start | bytes 388
  7.2 360.4 %reduce-scatter.4.cloned.1.call-start = ((), (), s32[]{:S(2)}) async-start(), calls=%async_computation.6 | async-start | bytes 8257536 | tf_op jit(solution)/shard_map/reduce_scatter | solution.py:100
  9.1 0.6 copy-start.8
  9.8 0.6 copy-start.6
  266.6 16.9 %copy-start = (bf16[2,3584,128]{2,1,0:T(8,128)(2,1)S(1)}, bf16[2,3584,128]{2,1,0:T(8,128)(2,1)}, u32[]{:S(2)}) copy-start(bf16[2,3584,128]{2,1,0:T(8,128)(2,1)} %param.11) | copy-start | bytes 5505028
  282.4 4.5 copy-start.15
  283.5 6.7 %copy-start.10 = (f32[512]{0:T(512)}, f32[512]{0:T(512)S(1)}, u32[]{:S(2)}) copy-start(f32[512]{0:T(512)S(1)} %convert_reduce_fusion.1) | copy-start | bytes 6148
  283.5 6.7 %slice-start = ((s8[7471104]{0:T(1024)(128)(4,1)}), s8[4194304]{0:T(1024)(128)(4,1)S(1)}, s32[]{:S(2)}) async-start(s8[7471104]{0:T(1024)(128)(4,1)} %bitcast.82), calls=%async_computation.8 | async-start | bytes 8388608
  286.9 3.4 slice-start.1
  286.9 3.5 copy-start.1
  291.5 1.1 copy-start.3
  291.5 37.1 %copy-start.19 = (bf16[512,128]{1,0:T(8,128)(2,1)}, bf16[512,128]{1,0:T(8,128)(2,1)S(1)}, u32[]{:S(2)}) copy-start(bf16[512,128]{1,0:T(8,128)(2,1)S(1)} %get-tuple-element.7) | copy-start | bytes 393220
  296.8 98.8 %reduce-scatter.6.cloned.1.call-start = ((), (), s32[]{:S(2)}) async-start(), calls=%async_computation.7 | async-start | bytes 8257536 | tf_op jit(solution)/shard_map/reduce_scatter | solution.py:100
  312.7 4.6 copy-start.16
  313.9 3.4 copy-start.12
  313.9 6.9 %slice-start.4 = ((s8[7471104]{0:T(1024)(128)(4,1)}), s8[4194304]{0:T(1024)(128)(4,1)S(1)}, s32[]{:S(2)}) async-start(s8[7471104]{0:T(1024)(128)(4,1)} %bitcast.86), calls=%async_computation.12 | async-start | bytes 8388608
  317.3 3.5 slice-start.5
  317.3 3.7 copy-start.2
  322.2 1.1 copy-start.4
  322.2 10.2 %copy-start.21 = (bf16[512,128]{1,0:T(8,128)(2,1)}, bf16[512,128]{1,0:T(8,128)(2,1)S(1)}, u32[]{:S(2)}) copy-start(bf16[512,128]{1,0:T(8,128)(2,1)S(1)} %get-tuple-element.10) | copy-start | bytes 393220
  327.4 0.7 copy-start.18
  327.4 1.5 copy-start.17
  362.3 39.7 %all-to-all-start.3 = ((f32[32,1,4]{2,1,0:T(1,128)}), f32[32,1,4]{2,1,0:T(1,128)S(1)}, u32[]{:S(2)}, u32[]{:S(2)}) async-start(f32[32,1,4]{2,1,0:T(1,128)} %bitcast.12), calls=%async_computation.5 | async-start | bytes 32768 | tf_op jit(solution)/shard_map/all_to_all | solution.py:112
  398.3 17.5 %slice-start.2 = ((s8[7471104]{0:T(1024)(128)(4,1)}), s8[3276800]{0:T(1024)(128)(4,1)S(1)}, s32[]{:S(2)}) async-start(s8[7471104]{0:T(1024)(128)(4,1)} %bitcast.84), calls=%async_computation.10 | async-start | bytes 6553600
  402.1 54.5 %all-to-all-start.2 = ((f32[32,2,2,3584]{3,2,1,0:T(2,128)}), f32[32,2,2,3584]{3,2,1,0:T(2,128)}, u32[]{:S(2)}, u32[]{:S(2)}) async-start(f32[32,2,2,3584]{3,2,1,0:T(2,128)} %pad_maximum_fusion), calls=%async_computation.4 | async-start | bytes 3670016 | tf_op jit(solution)/shard_map/all_to_all | solution.py:111
  412.3 3.4 slice-start.3
  412.4 4.6 slice-start.6
  415.8 2.4 slice-start.7
  418.1 1.2 copy-start.5
  419.3 1.2 copy-start.11
  419.3 1.2 copy-start.20
  420.5 0.9 copy-start.13
  420.5 0.9 copy-start.22
  423.8 3.5 copy-start.9
  426.0 33.1 %copy-start.7 = (f32[8,128]{1,0:T(8,128)S(1)}, f32[8,128]{1,0:T(8,128)}, u32[]{:S(2)}) copy-start(f32[8,128]{1,0:T(8,128)} %copy-done.6) | copy-start | bytes 12292
Sparse Core Ops, SparseCore 0:
  296.9 46.0 reduce-scatter.3
  345.6 49.9 reduce-scatter.5
